TPU v7x, 256 devices: a whole 4x4x8 slice. The times are simulated.
256 devices in a mesh: dp: 32 (over y, x, core), expert: 8 (over z).
Axes of the slice: x: 4, y: 4, z: 8, core: 2. Of those that a mesh axis runs over, the one named last changes fastest.
Arguments:
- tokens: bfloat16 [4096, 2048], P('dp'), may hold values from -6 to 6
- route_expert: int32 [4096, 4], P('dp'), may hold values from 0 to 31, all different within a row; in each aligned block of 128 rows (0 to 127, 128 to 255, ...) at most 32 rows name the same one
- route_weight: float32 [4096, 4], P('dp'), may hold values from 0.1 to 1
- gate_weight: bfloat16 [32, 1408, 2048], P('dp', 'expert'), may hold values from -0.125 to 0.125
- up_weight: bfloat16 [32, 1408, 2048], P('dp', 'expert'), may hold values from -0.125 to 0.125
- down_weight: bfloat16 [32, 1408, 2048], P('dp', 'expert'), may hold values from -0.15625 to 0.15625
- gate_scale: float32 [32, 1408], P('dp', 'expert'), may hold values from 0.5 to 2
- up_scale: float32 [32, 1408], P('dp', 'expert'), may hold values from 0.5 to 2
- down_scale: float32 [32, 2048], replicated, may hold values from 0.5 to 2
- cotangent: bfloat16 [4096, 2048], P('dp', 'expert'), may hold values from -6 to 6
Outputs:
- mixed: bfloat16 [4096, 2048], P('dp', 'expert')
- token_grad: bfloat16 [4096, 2048], P('dp', 'expert')
- route_grad: float32 [4096, 4], P('dp')
- gate_grad: float32 [32, 1408, 2048], P('dp', 'expert')
- up_grad: float32 [32, 1408, 2048], P('dp', 'expert')
- down_grad: float32 [32, 1408, 2048], P('dp', 'expert')
Inputs may be any that keep to these rules, and one draw needn't show every extreme that they name: `route_expert`: each row names 4 different experts. Among the 128 rows of one aligned block (the tokens of one index of dp) no expert is named by more than 32 rows, and in some block one expert is named by exactly 32 rows.
All inputs are finite; a program needn't handle non-finite values.
Results may differ from a plain program's by a relative error of at most 0.0058.
Values may be sent and summed in bfloat16 or wider, within the bound.
No kernel may reach another device: no remote copies, remote signals or barrier semaphores. Data moves between devices by JAX's collectives and lax.ppermute only.
A program may use at most 128 MiB of HBM per device.

v0:
```python
import jax
import jax.numpy as jnp
from jax import lax
from jax.sharding import PartitionSpec as P


def local(
    tokens,
    route_expert,
    route_weight,
    gate_weight,
    up_weight,
    down_weight,
    gate_scale,
    up_scale,
    down_scale,
    cotangent,
):
    owners = lax.axis_size("dp")
    tok_rows, width = tokens.shape
    choose = route_expert.shape[1]
    capacity = 2 * tok_rows * choose // owners
    slots = owners * capacity
    assigned = tok_rows * choose
    col_share = width // lax.axis_size("expert")
    col_start = lax.axis_index("expert") * col_share
    flat_expert = route_expert.reshape(-1)
    one_hot = (flat_expert[:, None] == jnp.arange(owners, dtype=jnp.int32)[None, :]).astype(
        jnp.int32
    )
    ranks = jnp.sum((jnp.cumsum(one_hot, axis=0) - 1) * one_hot, axis=1)
    slot_index = flat_expert * capacity + ranks
    slot_token = (
        jnp.zeros((slots,), jnp.int32)
        .at[slot_index]
        .set(jnp.arange(assigned, dtype=jnp.int32) // choose)
    )
    filled = jnp.zeros((slots,), jnp.bool_).at[slot_index].set(True)
    slot_weight = jnp.zeros((slots,), jnp.float32).at[slot_index].set(route_weight.reshape(-1))
    outgoing = jnp.where(
        filled[:, None], jnp.take(tokens, slot_token, axis=0), jnp.zeros((), tokens.dtype)
    )
    arrived = lax.all_to_all(
        outgoing.reshape(owners, capacity, width), "dp", split_axis=0, concat_axis=0, tiled=True
    ).reshape(slots, width)
    gate_local = gate_weight[0]
    up_local = up_weight[0]
    down_local = down_weight[0]
    gate_pre = (
        lax.dot_general(
            arrived, gate_local, (((1,), (1,)), ((), ())), preferred_element_type=jnp.float32
        )
        * gate_scale[0][None, :]
    )
    up_pre = (
        lax.dot_general(
            arrived, up_local, (((1,), (1,)), ((), ())), preferred_element_type=jnp.float32
        )
        * up_scale[0][None, :]
    )
    sigmoid_gate = jax.nn.sigmoid(gate_pre)
    silu_gate = gate_pre * sigmoid_gate
    hidden = (silu_gate * up_pre).astype(jnp.bfloat16)
    summed = lax.psum_scatter(
        lax.dot_general(
            down_local, hidden, (((0,), (1,)), ((), ())), preferred_element_type=jnp.float32
        ),
        "expert",
        scatter_dimension=0,
        tiled=True,
    )
    owner_scale = lax.dynamic_slice(down_scale, (lax.axis_index("dp"), col_start), (1, col_share))[
        0
    ]
    out_cols = (summed * owner_scale[:, None]).astype(jnp.bfloat16)
    returned = lax.all_to_all(
        out_cols.reshape(col_share, owners, capacity), "dp", split_axis=1, concat_axis=1, tiled=True
    ).reshape(col_share, slots)
    picked = (
        jnp.take(returned, slot_index, axis=1)
        .reshape(col_share, tok_rows, choose)
        .astype(jnp.float32)
    )
    mixed = jnp.sum(picked * route_weight[None, :, :], axis=2).T.astype(jnp.bfloat16)
    cot_cols = cotangent.T.astype(jnp.float32)
    route_part = jnp.sum(picked * cot_cols[:, :, None], axis=0)
    route_grad = lax.psum(route_part, "expert")
    slot_scale = jnp.repeat(down_scale, capacity, axis=0)
    full_cot = lax.all_gather(cotangent, "expert", axis=1, tiled=True)
    cot_slots = jnp.take(full_cot, slot_token, axis=0).astype(jnp.float32)
    weighted = (cot_slots * slot_weight[:, None] * slot_scale).astype(jnp.bfloat16)
    out_grad = lax.all_to_all(
        weighted.reshape(owners, capacity, width), "dp", split_axis=0, concat_axis=0, tiled=True
    ).reshape(slots, width)
    hidden_grad = lax.dot_general(
        out_grad, down_local, (((1,), (1,)), ((), ())), preferred_element_type=jnp.float32
    )
    gate_in = (
        hidden_grad
        * up_pre
        * sigmoid_gate
        * (1.0 + gate_pre * (1.0 - sigmoid_gate))
        * gate_scale[0][None, :]
    ).astype(jnp.bfloat16)
    up_in = (hidden_grad * silu_gate * up_scale[0][None, :]).astype(jnp.bfloat16)
    down_grad = lax.dot_general(
        hidden, out_grad, (((0,), (0,)), ((), ())), preferred_element_type=jnp.float32
    )
    gate_grad = lax.dot_general(
        gate_in, arrived, (((0,), (0,)), ((), ())), preferred_element_type=jnp.float32
    )
    up_grad = lax.dot_general(
        up_in, arrived, (((0,), (0,)), ((), ())), preferred_element_type=jnp.float32
    )
    first = lax.dot_general(
        gate_local, gate_in, (((0,), (1,)), ((), ())), preferred_element_type=jnp.float32
    )
    second = lax.dot_general(
        up_local, up_in, (((0,), (1,)), ((), ())), preferred_element_type=jnp.float32
    )
    input_cols = lax.psum_scatter(first + second, "expert", scatter_dimension=0, tiled=True)
    input_home = lax.all_to_all(
        input_cols.reshape(col_share, owners, capacity),
        "dp",
        split_axis=1,
        concat_axis=1,
        tiled=True,
    ).reshape(col_share, slots)
    token_grad = jnp.sum(
        jnp.take(input_home, slot_index, axis=1).reshape(col_share, tok_rows, choose), axis=2
    ).T.astype(jnp.bfloat16)
    return (mixed, token_grad, route_grad, gate_grad[None], up_grad[None], down_grad[None])


def solution(mesh):
    return jax.shard_map(
        local,
        mesh=mesh,
        in_specs=(
            P("dp", None),
            P("dp", None),
            P("dp", None),
            P("dp", "expert", None),
            P("dp", "expert", None),
            P("dp", "expert", None),
            P("dp", "expert"),
            P("dp", "expert"),
            P(),
            P("dp", "expert"),
        ),
        out_specs=(
            P("dp", "expert"),
            P("dp", "expert"),
            P("dp", None),
            P("dp", "expert", None),
            P("dp", "expert", None),
            P("dp", "expert", None),
        ),
        check_vma=False,
    )
```

profile of v0, /device:TPU:2, one launch (start us, length us, event | category | flops | bytes accessed | tf_op | source)
XLA Modules:
  0.0 436.8 jit_solution(8157642740581195982)
XLA Ops:
  7.2 0.0 copy-start
  7.2 0.9 copy.18
  8.0 0.1 eq.26
  8.2 0.1 reshape.136
  8.3 1.2 reduce-window.6
  9.5 0.2 slice_reduce_fusion
  9.7 0.1 mul.123
  9.8 0.1 fusion.11
  10.0 2.4 scatter_custom_fusion.1
  12.4 0.8 copy.22
  13.2 0.1 reshape.200
  13.3 29.3 %all_gather.3 = bf16[128,2048]{1,0:T(8,128)(2,1)S(1)} all-gather(bf16[128,256]{1,0:T(8,128)(2,1)} %param.21), channel_id=1, replica_groups=mesh['dp'=32,'expert'=8] {'expert'}, dimensions={1}, use_global_device_ids=true | all-gather | bytes 589824 | tf_op jit(solution)/shard_map/all_gather | solution.py:89
  42.7 2.4 scatter_custom_fusion.2
  45.1 0.0 copy-start.7
  45.1 6.0 %gather_fusion.3 = bf16[1024,2048]{1,0:T(8,128)(2,1)} fusion(bf16[128,2048]{1,0:T(8,128)(2,1)S(1)} %all_gather.3, s32[1024]{0:T(1024)S(1)} %fusion.13), kind=kCustom, calls=%fused_computation.1.clone | custom fusion | bytes 8392704 | tf_op jit(solution)/shard_map/jit(_take)/gather | solution.py:90
  51.2 0.0 copy-done.7
  51.2 4.5 %fusion = bf16[1024,2048]{1,0:T(8,128)(2,1)} fusion(bf16[1024,2048]{1,0:T(8,128)(2,1)} %gather_fusion.3, f32[32,2048]{1,0:T(8,128)S(1)} %copy-done.7, f32[1024]{0:T(1024)S(1)} %scatter_custom_fusion.2, pred[1024]{0:T(1024)(128)(4,1)S(1)} %compare_and_fusion.1), kind=kLoop, calls=%fused_computation.8 | loop fusion | flops 10485760 | bytes 8655872 | tf_op jit(solution)/shard_map/convert_element_type | solution.py:91
  55.6 7.8 %all-to-all-start.2 = ((bf16[32,32,2048]{2,1,0:T(8,128)(2,1)}), bf16[32,32,2048]{2,1,0:T(8,128)(2,1)}, u32[]{:S(2)}, u32[]{:S(2)}) async-start(bf16[32,32,2048]{2,1,0:T(8,128)(2,1)} %bitcast.93), calls=%async_computation.3 | async-start | bytes 8388608 | tf_op jit(solution)/shard_map/all_to_all | solution.py:92
  63.4 0.0 copy-done.1
  63.4 6.0 %gather_fusion.2 = bf16[1024,2048]{1,0:T(8,128)(2,1)} fusion(bf16[128,2048]{1,0:T(8,128)(2,1)S(1)} %copy-done.1, s32[1024]{0:T(1024)S(1)} %fusion.13), kind=kCustom, calls=%fused_computation.clone | custom fusion | bytes 8392704 | tf_op jit(solution)/shard_map/jit(_take)/gather | solution.py:41
  69.5 2.4 scatter_custom_fusion
  71.9 4.0 select_select_fusion
  75.9 38.9 %all-to-all-done.2 = bf16[32,32,2048]{2,1,0:T(8,128)(2,1)} async-done(((bf16[32,32,2048]{2,1,0:T(8,128)(2,1)}), bf16[32,32,2048]{2,1,0:T(8,128)(2,1)}, u32[]{:S(2)}, u32[]{:S(2)}) %all-to-all-start.2) | async-done | bytes 4194336 | tf_op jit(solution)/shard_map/all_to_all | solution.py:92
  114.9 7.4 %all-to-all-start = ((bf16[32,32,2048]{2,1,0:T(8,128)(2,1)}), bf16[32,32,2048]{2,1,0:T(8,128)(2,1)}, u32[]{:S(2)}, u32[]{:S(2)}) async-start(bf16[32,32,2048]{2,1,0:T(8,128)(2,1)} %bitcast.92), calls=%async_computation | async-start | bytes 8388608 | tf_op jit(solution)/shard_map/all_to_all | solution.py:43
  122.3 0.0 copy-start.6
  122.3 0.0 copy-start.9
  122.3 0.2 reduce-scatter.3.cloned.1.call-start
  122.5 4.6 %fusion.1 = f32[1024,176]{0,1:T(8,128)} fusion(bf16[1024,2048]{1,0:T(8,128)(2,1)} %bitcast.18, bf16[1,176,2048]{2,1,0:T(8,128)(2,1)S(1)} %copy-done.5), kind=kOutput, calls=%fused_computation.18 | convolution fusion | flops 738197504 | bytes 5636096 | tf_op jit(solution)/shard_map/dot_general | solution.py:95
  127.1 46.7 %all-to-all-done = bf16[32,32,2048]{2,1,0:T(8,128)(2,1)} async-done(((bf16[32,32,2048]{2,1,0:T(8,128)(2,1)}), bf16[32,32,2048]{2,1,0:T(8,128)(2,1)}, u32[]{:S(2)}, u32[]{:S(2)}) %all-to-all-start) | async-done | bytes 4194336 | tf_op jit(solution)/shard_map/all_to_all | solution.py:43
  173.8 3.8 convolution_multiply_fusion.1
  177.6 4.0 multiply_convert_fusion.3
  181.7 0.0 copy-start.2
  181.7 0.0 copy-start.3
  181.7 0.7 copy-done.2
  182.4 4.5 %convolution_bitcast_fusion = f32[2048,1024]{0,1:T(8,128)} fusion(bf16[1024,176]{0,1:T(8,128)(2,1)S(1)} %get-tuple-element.15, bf16[1,176,2048]{2,1,0:T(8,128)(2,1)S(1)} %copy-done.5), kind=kOutput, calls=%fused_computation.10 | convolution fusion | flops 738197504 | bytes 9469952 | tf_op jit(solution)/shard_map/dot_general | solution.py:65
  186.9 0.0 reduce-scatter.3.cloned.1.call-update
  186.9 0.0 reduce-scatter.5.cloned.1.call-start
  187.0 1.3 fusion.6
  188.3 4.5 %add_bitcast_fusion = f32[2048,1024]{0,1:T(8,128)} fusion(f32[1024,2048]{1,0:T(8,128)S(1)} %fusion.6, bf16[1024,176]{0,1:T(8,128)(2,1)S(1)} %get-tuple-element.17, bf16[1,176,2048]{2,1,0:T(8,128)(2,1)S(1)} %copy-done), kind=kOutput, calls=%fused_computation.9 | convolution fusion | flops 740294656 | bytes 17858560 | tf_op jit(solution)/shard_map/dot_general | solution.py:118
  192.8 0.0 reduce-scatter.5.cloned.1.call-update
  192.8 0.1 reduce_sum.43
  192.9 0.1 dynamic_slice.3
  193.0 85.6 %reduce-scatter.3.cloned.1.call-done = f32[256,1024]{0,1:T(8,128)} async-done(((f32[2048,1024]{0,1:T(8,128)}), f32[256,1024]{0,1:T(8,128)}) %reduce-scatter.3.cloned.1.call-update) | async-done | bytes 1048592 | tf_op jit(solution)/shard_map/reduce_scatter | solution.py:64
  278.6 2.1 multiply_convert_fusion
  280.7 7.4 %all-to-all-start.1 = ((bf16[256,32,32]{0,2,1:T(8,128)(2,1)}), bf16[256,32,32]{0,2,1:T(8,128)(2,1)S(1)}, u32[]{:S(2)}, u32[]{:S(2)}) async-start(bf16[256,32,32]{0,2,1:T(8,128)(2,1)} %bitcast.12), calls=%async_computation.2 | async-start | bytes 1048576 | tf_op jit(solution)/shard_map/all_to_all | solution.py:76
  288.1 0.1 broadcast_in_dim.87
  288.3 0.1 mul.148
  288.4 0.2 mul.149
  288.6 86.1 %reduce-scatter.5.cloned.1.call-done = f32[256,1024]{0,1:T(8,128)} async-done(((f32[2048,1024]{0,1:T(8,128)}), f32[256,1024]{0,1:T(8,128)}) %reduce-scatter.5.cloned.1.call-update) | async-done | bytes 1048592 | tf_op jit(solution)/shard_map/reduce_scatter | solution.py:121
  374.7 0.0 all-to-all-done.1
  374.7 7.4 %all-to-all-start.3 = ((f32[256,32,32]{0,2,1:T(8,128)}), f32[256,32,32]{0,2,1:T(8,128)S(1)}, u32[]{:S(2)}, u32[]{:S(2)}) async-start(f32[256,32,32]{0,2,1:T(8,128)} %bitcast.97), calls=%async_computation.5 | async-start | bytes 2097152 | tf_op jit(solution)/shard_map/all_to_all | solution.py:122
  382.2 4.3 convolution_bitcast_fusion.1
  386.5 4.3 convolution_bitcast_fusion.3
  390.8 4.2 convolution_bitcast_fusion.2
  395.0 1.9 gather_fusion
  397.0 0.1 gather.16
  397.0 0.2 multiply_reduce_fusion
  397.3 0.1 reduce_sum.48
  397.4 28.7 %psum.7 = f32[128,4]{1,0:T(8,128)S(1)} all-reduce(f32[128,4]{1,0:T(8,128)S(1)} %reduce_sum.48), channel_id=1, replica_groups=mesh['dp'=32,'expert'=8] {'expert'}, use_global_device_ids=true, to_apply=%region_11.13 | all-reduce | flops 512 | bytes 4096 | tf_op jit(solution)/shard_map/psum | solution.py:87
  426.1 0.7 copy.24
  426.7 0.0 all-to-all-done.3
  426.7 1.6 gather_fusion.1
  428.3 0.1 gather.18
  428.5 1.4 select_reduce_fusion
  (27 shorter events, 0.2 us)
Async XLA Ops:
  7.2 170.4 %copy-start = (bf16[1,176,2048]{2,1,0:T(8,128)(2,1)S(1)}, bf16[1,176,2048]{2,1,0:T(8,128)(2,1)}, u32[]{:S(2)}) copy-start(bf16[1,176,2048]{2,1,0:T(8,128)(2,1)} %param.16) | copy-start | bytes 2162692
  45.1 6.0 %copy-start.7 = (f32[32,2048]{1,0:T(8,128)S(1)}, f32[32,2048]{1,0:T(8,128)}, u32[]{:S(2)}) copy-start(f32[32,2048]{1,0:T(8,128)} %param.20) | copy-start | bytes 786436
  55.6 7.8 %copy-start.1 = (bf16[128,2048]{1,0:T(8,128)(2,1)S(1)}, bf16[128,2048]{1,0:T(8,128)(2,1)}, u32[]{:S(2)}) copy-start(bf16[128,2048]{1,0:T(8,128)(2,1)} %param.12) | copy-start | bytes 1572868
  55.6 59.2 %all-to-all-start.2 = ((bf16[32,32,2048]{2,1,0:T(8,128)(2,1)}), bf16[32,32,2048]{2,1,0:T(8,128)(2,1)}, u32[]{:S(2)}, u32[]{:S(2)}) async-start(bf16[32,32,2048]{2,1,0:T(8,128)(2,1)} %bitcast.93), calls=%async_computation.3 | async-start | bytes 8388608 | tf_op jit(solution)/shard_map/all_to_all | solution.py:92
  114.9 7.7 %copy-start.5 = (bf16[1,176,2048]{2,1,0:T(8,128)(2,1)S(1)}, bf16[1,176,2048]{2,1,0:T(8,128)(2,1)}, u32[]{:S(2)}) copy-start(bf16[1,176,2048]{2,1,0:T(8,128)(2,1)} %param.17) | copy-start | bytes 2162692
  114.9 58.9 %all-to-all-start = ((bf16[32,32,2048]{2,1,0:T(8,128)(2,1)}), bf16[32,32,2048]{2,1,0:T(8,128)(2,1)}, u32[]{:S(2)}, u32[]{:S(2)}) async-start(bf16[32,32,2048]{2,1,0:T(8,128)(2,1)} %bitcast.92), calls=%async_computation | async-start | bytes 8388608 | tf_op jit(solution)/shard_map/all_to_all | solution.py:43
  122.3 51.5 %copy-start.6 = (bf16[1,176,2048]{2,1,0:T(8,128)(2,1)S(1)}, bf16[1,176,2048]{2,1,0:T(8,128)(2,1)}, u32[]{:S(2)}) copy-start(bf16[1,176,2048]{2,1,0:T(8,128)(2,1)} %param.15) | copy-start | bytes 2162692
  122.3 51.5 %copy-start.9 = (f32[1,176]{1,0:T(1,128)S(1)}, f32[1,176]{1,0:T(1,128)}, u32[]{:S(2)}) copy-start(f32[1,176]{1,0:T(1,128)} %param.18) | copy-start | bytes 2116
  122.3 156.3 %reduce-scatter.3.cloned.1.call-start = ((), (), s32[]{:S(2)}) async-start(), calls=%async_computation.6 | async-start | bytes 9437184 | tf_op jit(solution)/shard_map/reduce_scatter | solution.py:64
  127.1 50.5 %copy-start.10 = (f32[1,176]{1,0:T(1,128)S(1)}, f32[1,176]{1,0:T(1,128)}, u32[]{:S(2)}) copy-start(f32[1,176]{1,0:T(1,128)} %param.19) | copy-start | bytes 2116
  173.8 3.8 copy-start.11
  181.7 0.7 copy-start.2
  181.7 6.6 %copy-start.3 = (bf16[1024,176]{0,1:T(8,128)(2,1)}, bf16[1024,176]{0,1:T(8,128)(2,1)S(1)}, u32[]{:S(2)}) copy-start(bf16[1024,176]{0,1:T(8,128)(2,1)S(1)} %get-tuple-element.17) | copy-start | bytes 1081348
  186.9 187.8 %reduce-scatter.5.cloned.1.call-start = ((), (), s32[]{:S(2)}) async-start(), calls=%async_computation.7 | async-start | bytes 9437184 | tf_op jit(solution)/shard_map/reduce_scatter | solution.py:121
  192.8 95.5 %copy-start.8 = (bf16[128,256]{1,0:T(8,128)(2,1)S(1)}, bf16[128,256]{1,0:T(8,128)(2,1)}, u32[]{:S(2)}) copy-start(bf16[128,256]{1,0:T(8,128)(2,1)} %param.21) | copy-start | bytes 196612
  280.7 94.0 %all-to-all-start.1 = ((bf16[256,32,32]{0,2,1:T(8,128)(2,1)}), bf16[256,32,32]{0,2,1:T(8,128)(2,1)S(1)}, u32[]{:S(2)}, u32[]{:S(2)}) async-start(bf16[256,32,32]{0,2,1:T(8,128)(2,1)} %bitcast.12), calls=%async_computation.2 | async-start | bytes 1048576 | tf_op jit(solution)/shard_map/all_to_all | solution.py:76
  374.7 52.0 %all-to-all-start.3 = ((f32[256,32,32]{0,2,1:T(8,128)}), f32[256,32,32]{0,2,1:T(8,128)S(1)}, u32[]{:S(2)}, u32[]{:S(2)}) async-start(f32[256,32,32]{0,2,1:T(8,128)} %bitcast.97), calls=%async_computation.5 | async-start | bytes 2097152 | tf_op jit(solution)/shard_map/all_to_all | solution.py:122
  386.5 4.3 copy-start.4
Sparse Core Ops, SparseCore 0:
  187.0 91.5 reduce-scatter.2
  281.1 93.5 reduce-scatter.4
where the time goes:
time: 437 us
  waiting for transfers between devices  257 us (59%)
  blocking collectives  58 us (13%)
  matrix products  35.5 us (8%)
  starting transfers between devices  30.3 us (7%)
  local copies, waits for them, and re-layouts  27.5 us (6%)
  between operations  14.4 us (3%)
  other arithmetic  13.6 us (3%)
    reduce_scatter x1, waiting for transfers between devices, local(): lax.psum_scatter(first + second, 'expert', scatter_dimension=0, tiled=True)  86.1 us
    reduce_scatter x1, waiting for transfers between devices, local(): lax.psum_scatter(lax.dot_general(down_local, hidden, (((0,), (1,)), ((),...  85.6 us
    all_to_all x1, waiting for transfers between devices, local(): lax.all_to_all(outgoing.reshape(owners, capacity, width), 'dp', split_axi...  46.7 us
    all_to_all x1, waiting for transfers between devices, local(): lax.all_to_all(weighted.reshape(owners, capacity, width), 'dp', split_axi...  38.9 us
    all_gather x1, blocking collectives, local(): full_cot = lax.all_gather(cotangent, 'expert', axis=1, tiled=True)  29.3 us
    psum x1, blocking collectives, local(): route_grad = lax.psum(route_part, 'expert')  28.7 us
  transfers between devices with their start and end apart: 6, of which 4 were waited for; matrix products, arithmetic and copies ran while one was open for 9% of the time, Pallas kernels for 0%

commit v1 on v0

--- a/solution.py
+++ b/solution.py
@@ -84,7 +84,11 @@
     mixed = jnp.sum(picked * route_weight[None, :, :], axis=2).T.astype(jnp.bfloat16)
     cot_cols = cotangent.T.astype(jnp.float32)
     route_part = jnp.sum(picked * cot_cols[:, :, None], axis=0)
-    route_grad = lax.psum(route_part, "expert")
+    route_grad = route_part
+    for hop in (1, 2, 4):
+        route_grad = route_grad + lax.ppermute(
+            route_grad, "expert", [(dev, dev ^ hop) for dev in range(8)]
+        )
     slot_scale = jnp.repeat(down_scale, capacity, axis=0)
     full_cot = lax.all_gather(cotangent, "expert", axis=1, tiled=True)
     cot_slots = jnp.take(full_cot, slot_token, axis=0).astype(jnp.float32)

time: 437 us -> 417 us (0.954)
  blocking collectives: 58 us -> 29.3 us
  starting transfers between devices: 30.3 us -> 37.2 us
    psum x1 -> x0, blocking collectives: 28.7 us -> none  [local(): route_grad = lax.psum(route_part, 'expert')]
    ppermute x0 -> x3, starting transfers between devices: none -> 6.84 us  [local(): lax.ppermute(route_grad, 'expert', [(dev, dev ^ hop) for dev in range(8)])]
  transfers between devices with their start and end apart: 6 -> 9, of which waited for: 4 -> 5; matrix products, arithmetic and copies ran while one was open for 9% -> 10% of each run, Pallas kernels for 0% -> 0%
where the time goes in v1:
time: 417 us; the launch traced here: 416 us
  waiting for transfers between devices  259 us (62%)
  starting transfers between devices  37.2 us (9%)
  matrix products  35.4 us (8%)
  blocking collectives  29.3 us (7%)
  local copies, waits for them, and re-layouts  27.5 us (7%)
  between operations  14.4 us (3%)
  other arithmetic  13.7 us (3%)
    reduce_scatter x1, waiting for transfers between devices, local(): lax.psum_scatter(first + second, 'expert', scatter_dimension=0, tiled=True)  86.1 us
    reduce_scatter x1, waiting for transfers between devices, local(): lax.psum_scatter(lax.dot_general(down_local, hidden, (((0,), (1,)), ((),...  85.6 us
    all_to_all x1, waiting for transfers between devices, local(): lax.all_to_all(outgoing.reshape(owners, capacity, width), 'dp', split_axi...  46.7 us
    all_to_all x1, waiting for transfers between devices, local(): lax.all_to_all(weighted.reshape(owners, capacity, width), 'dp', split_axi...  38.9 us
    all_gather x1, blocking collectives, local(): full_cot = lax.all_gather(cotangent, 'expert', axis=1, tiled=True)  29.3 us
  transfers between devices with their start and end apart: 9, of which 5 were waited for; matrix products, arithmetic and copies ran while one was open for 10% of the time, Pallas kernels for 0%

profile of v1, /device:TPU:2, one launch (start us, length us, event | category | flops | bytes accessed | tf_op | source)
XLA Modules:
  0.0 416.1 jit_solution(18142154918511861397)
XLA Ops:
  7.2 0.0 copy-start
  7.2 0.9 copy.18
  8.0 0.1 eq.26
  8.2 0.1 reshape.136
  8.3 1.2 reduce-window.6
  9.5 0.2 slice_reduce_fusion
  9.7 0.1 mul.123
  9.8 0.1 fusion.11
  10.0 2.4 scatter_custom_fusion.1
  12.4 0.8 copy.22
  13.2 0.1 reshape.200
  13.3 29.3 %all_gather.3 = bf16[128,2048]{1,0:T(8,128)(2,1)S(1)} all-gather(bf16[128,256]{1,0:T(8,128)(2,1)} %param.21), channel_id=1, replica_groups=mesh['dp'=32,'expert'=8] {'expert'}, dimensions={1}, use_global_device_ids=true | all-gather | bytes 589824 | tf_op jit(solution)/shard_map/all_gather | solution.py:93
  42.7 2.4 scatter_custom_fusion.2
  45.1 0.0 copy-start.7
  45.1 6.0 %gather_fusion.3 = bf16[1024,2048]{1,0:T(8,128)(2,1)} fusion(bf16[128,2048]{1,0:T(8,128)(2,1)S(1)} %all_gather.3, s32[1024]{0:T(1024)S(1)} %fusion.13), kind=kCustom, calls=%fused_computation.1.clone | custom fusion | bytes 8392704 | tf_op jit(solution)/shard_map/jit(_take)/gather | solution.py:94
  51.2 4.5 %fusion = bf16[1024,2048]{1,0:T(8,128)(2,1)} fusion(bf16[1024,2048]{1,0:T(8,128)(2,1)} %gather_fusion.3, f32[32,2048]{1,0:T(8,128)S(1)} %copy-done.7, f32[1024]{0:T(1024)S(1)} %scatter_custom_fusion.2, pred[1024]{0:T(1024)(128)(4,1)S(1)} %compare_and_fusion.1), kind=kLoop, calls=%fused_computation.8 | loop fusion | flops 10485760 | bytes 8655872 | tf_op jit(solution)/shard_map/convert_element_type | solution.py:95
  55.6 7.8 %all-to-all-start.2 = ((bf16[32,32,2048]{2,1,0:T(8,128)(2,1)}), bf16[32,32,2048]{2,1,0:T(8,128)(2,1)}, u32[]{:S(2)}, u32[]{:S(2)}) async-start(bf16[32,32,2048]{2,1,0:T(8,128)(2,1)} %bitcast.93), calls=%async_computation.3 | async-start | bytes 8388608 | tf_op jit(solution)/shard_map/all_to_all | solution.py:96
  63.4 6.0 %gather_fusion.2 = bf16[1024,2048]{1,0:T(8,128)(2,1)} fusion(bf16[128,2048]{1,0:T(8,128)(2,1)S(1)} %copy-done.1, s32[1024]{0:T(1024)S(1)} %fusion.13), kind=kCustom, calls=%fused_computation.clone | custom fusion | bytes 8392704 | tf_op jit(solution)/shard_map/jit(_take)/gather | solution.py:41
  69.5 2.4 scatter_custom_fusion
  71.9 4.0 select_select_fusion
  75.9 38.9 %all-to-all-done.2 = bf16[32,32,2048]{2,1,0:T(8,128)(2,1)} async-done(((bf16[32,32,2048]{2,1,0:T(8,128)(2,1)}), bf16[32,32,2048]{2,1,0:T(8,128)(2,1)}, u32[]{:S(2)}, u32[]{:S(2)}) %all-to-all-start.2) | async-done | bytes 4194336 | tf_op jit(solution)/shard_map/all_to_all | solution.py:96
  114.9 7.4 %all-to-all-start = ((bf16[32,32,2048]{2,1,0:T(8,128)(2,1)}), bf16[32,32,2048]{2,1,0:T(8,128)(2,1)}, u32[]{:S(2)}, u32[]{:S(2)}) async-start(bf16[32,32,2048]{2,1,0:T(8,128)(2,1)} %bitcast.92), calls=%async_computation | async-start | bytes 8388608 | tf_op jit(solution)/shard_map/all_to_all | solution.py:43
  122.3 0.0 copy-start.6
  122.3 0.0 copy-start.9
  122.3 0.2 reduce-scatter.3.cloned.1.call-start
  122.5 4.6 %fusion.1 = f32[1024,176]{0,1:T(8,128)} fusion(bf16[1024,2048]{1,0:T(8,128)(2,1)} %bitcast.18, bf16[1,176,2048]{2,1,0:T(8,128)(2,1)S(1)} %copy-done.5), kind=kOutput, calls=%fused_computation.18 | convolution fusion | flops 738197504 | bytes 5636096 | tf_op jit(solution)/shard_map/dot_general | solution.py:99
  127.1 46.7 %all-to-all-done = bf16[32,32,2048]{2,1,0:T(8,128)(2,1)} async-done(((bf16[32,32,2048]{2,1,0:T(8,128)(2,1)}), bf16[32,32,2048]{2,1,0:T(8,128)(2,1)}, u32[]{:S(2)}, u32[]{:S(2)}) %all-to-all-start) | async-done | bytes 4194336 | tf_op jit(solution)/shard_map/all_to_all | solution.py:43
  173.8 3.8 convolution_multiply_fusion.1
  177.6 4.0 multiply_convert_fusion.3
  181.7 0.0 copy-start.2
  181.7 0.0 copy-start.3
  181.7 0.7 copy-done.2
  182.4 4.5 %convolution_bitcast_fusion = f32[2048,1024]{0,1:T(8,128)} fusion(bf16[1024,176]{0,1:T(8,128)(2,1)S(1)} %get-tuple-element.15, bf16[1,176,2048]{2,1,0:T(8,128)(2,1)S(1)} %copy-done.5), kind=kOutput, calls=%fused_computation.10 | convolution fusion | flops 738197504 | bytes 9469952 | tf_op jit(solution)/shard_map/dot_general | solution.py:65
  186.9 0.0 reduce-scatter.3.cloned.1.call-update
  186.9 0.0 reduce-scatter.5.cloned.1.call-start
  187.0 1.3 fusion.6
  188.3 4.5 %add_bitcast_fusion = f32[2048,1024]{0,1:T(8,128)} fusion(f32[1024,2048]{1,0:T(8,128)S(1)} %fusion.6, bf16[1024,176]{0,1:T(8,128)(2,1)S(1)} %get-tuple-element.17, bf16[1,176,2048]{2,1,0:T(8,128)(2,1)S(1)} %copy-done), kind=kOutput, calls=%fused_computation.9 | convolution fusion | flops 740294656 | bytes 17858560 | tf_op jit(solution)/shard_map/dot_general | solution.py:122
  192.8 0.0 reduce-scatter.5.cloned.1.call-update
  192.8 0.1 reduce_sum.43
  192.9 0.1 dynamic_slice.3
  193.0 85.6 %reduce-scatter.3.cloned.1.call-done = f32[256,1024]{0,1:T(8,128)} async-done(((f32[2048,1024]{0,1:T(8,128)}), f32[256,1024]{0,1:T(8,128)}) %reduce-scatter.3.cloned.1.call-update) | async-done | bytes 1048592 | tf_op jit(solution)/shard_map/reduce_scatter | solution.py:64
  278.6 2.1 multiply_convert_fusion
  280.7 7.4 %all-to-all-start.1 = ((bf16[256,32,32]{0,2,1:T(8,128)(2,1)}), bf16[256,32,32]{0,2,1:T(8,128)(2,1)S(1)}, u32[]{:S(2)}, u32[]{:S(2)}) async-start(bf16[256,32,32]{0,2,1:T(8,128)(2,1)} %bitcast.12), calls=%async_computation.2 | async-start | bytes 1048576 | tf_op jit(solution)/shard_map/all_to_all | solution.py:76
  288.1 0.1 broadcast_in_dim.87
  288.3 0.1 mul.148
  288.4 0.2 mul.149
  288.6 86.1 %reduce-scatter.5.cloned.1.call-done = f32[256,1024]{0,1:T(8,128)} async-done(((f32[2048,1024]{0,1:T(8,128)}), f32[256,1024]{0,1:T(8,128)}) %reduce-scatter.5.cloned.1.call-update) | async-done | bytes 1048592 | tf_op jit(solution)/shard_map/reduce_scatter | solution.py:125
  374.7 7.4 %all-to-all-start.3 = ((f32[256,32,32]{0,2,1:T(8,128)}), f32[256,32,32]{0,2,1:T(8,128)S(1)}, u32[]{:S(2)}, u32[]{:S(2)}) async-start(f32[256,32,32]{0,2,1:T(8,128)} %bitcast.97), calls=%async_computation.5 | async-start | bytes 2097152 | tf_op jit(solution)/shard_map/all_to_all | solution.py:126
  382.2 2.0 gather_fusion
  384.1 0.2 multiply_reduce_fusion
  384.4 0.1 reduce_sum.48
  384.5 0.1 collective-permute-start
  384.6 4.3 %convolution_bitcast_fusion.1 = f32[1,176,2048]{2,1,0:T(8,128)} fusion(bf16[1024,176]{0,1:T(8,128)(2,1)} %copy-done.2, bf16[1024,2048]{1,0:T(8,128)(2,1)} %bitcast.18), kind=kOutput, calls=%fused_computation.12 | convolution fusion | flops 738197504 | bytes 5996544 | tf_op jit(solution)/shard_map/dot_general | solution.py:110
  388.9 3.8 collective-permute-start.1
  392.8 4.2 %convolution_bitcast_fusion.3 = f32[1,176,2048]{2,1,0:T(8,128)} fusion(bf16[1024,176]{0,1:T(8,128)(2,1)S(1)} %get-tuple-element.16, bf16[1024,2048]{1,0:T(8,128)(2,1)} %bitcast.4), kind=kOutput, calls=%fused_computation.14 | convolution fusion | flops 738197504 | bytes 5996544 | tf_op jit(solution)/shard_map/dot_general | solution.py:113
  397.0 0.0 collective-permute-done.1
  397.0 2.9 collective-permute-start.2
  399.9 4.2 %convolution_bitcast_fusion.2 = f32[1,176,2048]{2,1,0:T(8,128)} fusion(bf16[1024,176]{0,1:T(8,128)(2,1)S(1)} %copy-done.4, bf16[1024,2048]{1,0:T(8,128)(2,1)} %bitcast.4), kind=kOutput, calls=%fused_computation.13 | convolution fusion | flops 738197504 | bytes 5996544 | tf_op jit(solution)/shard_map/dot_general | solution.py:116
  404.1 0.1 gather.16
  404.2 1.3 collective-permute-done.2
  405.5 0.7 copy.24
  406.1 1.6 gather_fusion.1
  407.7 0.1 gather.18
  407.8 1.4 select_reduce_fusion
  (35 shorter events, 0.2 us)
Async XLA Ops:
  7.2 170.4 %copy-start = (bf16[1,176,2048]{2,1,0:T(8,128)(2,1)S(1)}, bf16[1,176,2048]{2,1,0:T(8,128)(2,1)}, u32[]{:S(2)}) copy-start(bf16[1,176,2048]{2,1,0:T(8,128)(2,1)} %param.16) | copy-start | bytes 2162692
  45.1 6.0 %copy-start.7 = (f32[32,2048]{1,0:T(8,128)S(1)}, f32[32,2048]{1,0:T(8,128)}, u32[]{:S(2)}) copy-start(f32[32,2048]{1,0:T(8,128)} %param.20) | copy-start | bytes 786436
  55.6 7.8 %copy-start.1 = (bf16[128,2048]{1,0:T(8,128)(2,1)S(1)}, bf16[128,2048]{1,0:T(8,128)(2,1)}, u32[]{:S(2)}) copy-start(bf16[128,2048]{1,0:T(8,128)(2,1)} %param.12) | copy-start | bytes 1572868
  55.6 59.2 %all-to-all-start.2 = ((bf16[32,32,2048]{2,1,0:T(8,128)(2,1)}), bf16[32,32,2048]{2,1,0:T(8,128)(2,1)}, u32[]{:S(2)}, u32[]{:S(2)}) async-start(bf16[32,32,2048]{2,1,0:T(8,128)(2,1)} %bitcast.93), calls=%async_computation.3 | async-start | bytes 8388608 | tf_op jit(solution)/shard_map/all_to_all | solution.py:96
  114.9 7.7 %copy-start.5 = (bf16[1,176,2048]{2,1,0:T(8,128)(2,1)S(1)}, bf16[1,176,2048]{2,1,0:T(8,128)(2,1)}, u32[]{:S(2)}) copy-start(bf16[1,176,2048]{2,1,0:T(8,128)(2,1)} %param.17) | copy-start | bytes 2162692
  114.9 58.9 %all-to-all-start = ((bf16[32,32,2048]{2,1,0:T(8,128)(2,1)}), bf16[32,32,2048]{2,1,0:T(8,128)(2,1)}, u32[]{:S(2)}, u32[]{:S(2)}) async-start(bf16[32,32,2048]{2,1,0:T(8,128)(2,1)} %bitcast.92), calls=%async_computation | async-start | bytes 8388608 | tf_op jit(solution)/shard_map/all_to_all | solution.py:43
  122.3 51.5 %copy-start.6 = (bf16[1,176,2048]{2,1,0:T(8,128)(2,1)S(1)}, bf16[1,176,2048]{2,1,0:T(8,128)(2,1)}, u32[]{:S(2)}) copy-start(bf16[1,176,2048]{2,1,0:T(8,128)(2,1)} %param.15) | copy-start | bytes 2162692
  122.3 51.5 %copy-start.9 = (f32[1,176]{1,0:T(1,128)S(1)}, f32[1,176]{1,0:T(1,128)}, u32[]{:S(2)}) copy-start(f32[1,176]{1,0:T(1,128)} %param.18) | copy-start | bytes 2116
  122.3 156.3 %reduce-scatter.3.cloned.1.call-start = ((), (), s32[]{:S(2)}) async-start(), calls=%async_computation.6 | async-start | bytes 9437184 | tf_op jit(solution)/shard_map/reduce_scatter | solution.py:64
  127.1 50.5 %copy-start.10 = (f32[1,176]{1,0:T(1,128)S(1)}, f32[1,176]{1,0:T(1,128)}, u32[]{:S(2)}) copy-start(f32[1,176]{1,0:T(1,128)} %param.19) | copy-start | bytes 2116
  173.8 3.8 copy-start.11
  181.7 0.7 copy-start.2
  181.7 6.6 %copy-start.3 = (bf16[1024,176]{0,1:T(8,128)(2,1)}, bf16[1024,176]{0,1:T(8,128)(2,1)S(1)}, u32[]{:S(2)}) copy-start(bf16[1024,176]{0,1:T(8,128)(2,1)S(1)} %get-tuple-element.17) | copy-start | bytes 1081348
  186.9 187.8 %reduce-scatter.5.cloned.1.call-start = ((), (), s32[]{:S(2)}) async-start(), calls=%async_computation.7 | async-start | bytes 9437184 | tf_op jit(solution)/shard_map/reduce_scatter | solution.py:125
  192.8 95.5 %copy-start.8 = (bf16[128,256]{1,0:T(8,128)(2,1)S(1)}, bf16[128,256]{1,0:T(8,128)(2,1)}, u32[]{:S(2)}) copy-start(bf16[128,256]{1,0:T(8,128)(2,1)} %param.21) | copy-start | bytes 196612
  280.7 94.0 %all-to-all-start.1 = ((bf16[256,32,32]{0,2,1:T(8,128)(2,1)}), bf16[256,32,32]{0,2,1:T(8,128)(2,1)S(1)}, u32[]{:S(2)}, u32[]{:S(2)}) async-start(bf16[256,32,32]{0,2,1:T(8,128)(2,1)} %bitcast.12), calls=%async_computation.2 | async-start | bytes 1048576 | tf_op jit(solution)/shard_map/all_to_all | solution.py:76
  374.7 31.4 %all-to-all-start.3 = ((f32[256,32,32]{0,2,1:T(8,128)}), f32[256,32,32]{0,2,1:T(8,128)S(1)}, u32[]{:S(2)}, u32[]{:S(2)}) async-start(f32[256,32,32]{0,2,1:T(8,128)} %bitcast.97), calls=%async_computation.5 | async-start | bytes 2097152 | tf_op jit(solution)/shard_map/all_to_all | solution.py:126
  384.5 4.4 %collective-permute-start = (f32[128,4]{1,0:T(8,128)S(1)}, f32[128,4]{1,0:T(8,128)S(1)}, u32[]{:S(2)}, u32[]{:S(2)}) collective-permute-start(f32[128,4]{1,0:T(8,128)S(1)} %reduce_sum.48), channel_id=1, source_target_pairs={{0,1},{1,0},{2,3},{3,2},{4,5},{5,4},{6,7},{7,6},{8,9},{9,8},{10,11... | collective-permute-start | bytes 6152 | tf_op jit(solution)/shard_map/ppermute | solution.py:89
  388.9 11.0 %copy-start.4 = (bf16[1024,176]{0,1:T(8,128)(2,1)S(1)}, bf16[1024,176]{0,1:T(8,128)(2,1)}, u32[]{:S(2)}) copy-start(bf16[1024,176]{0,1:T(8,128)(2,1)} %copy-done.3) | copy-start | bytes 1081348
  388.9 8.0 %collective-permute-start.1 = (f32[128,4]{1,0:T(8,128)S(1)}, f32[128,4]{1,0:T(8,128)S(1)}, u32[]{:S(2)}, u32[]{:S(2)}) collective-permute-start(f32[128,4]{1,0:T(8,128)S(1)} %add.97), channel_id=1, source_target_pairs={{0,2},{1,3},{2,0},{3,1},{4,6},{5,7},{6,4},{7,5},{8,10},{9,11},{10,... | collective-permute-start | bytes 6152 | tf_op jit(solution)/shard_map/ppermute | solution.py:89
  397.0 8.4 %collective-permute-start.2 = (f32[128,4]{1,0:T(8,128)S(1)}, f32[128,4]{1,0:T(8,128)S(1)}, u32[]{:S(2)}, u32[]{:S(2)}) collective-permute-start(f32[128,4]{1,0:T(8,128)S(1)} %add.98), channel_id=1, source_target_pairs={{0,4},{1,5},{2,6},{3,7},{4,0},{5,1},{6,2},{7,3},{8,12},{9,13},{10,... | collective-permute-start | bytes 6152 | tf_op jit(solution)/shard_map/ppermute | solution.py:89
Sparse Core Ops, SparseCore 0:
  187.0 91.5 reduce-scatter.2
  281.1 93.5 reduce-scatter.4
